TPU v7x, 512 devices: a whole 4x8x8 slice. The times are simulated.
512 devices in a mesh: section: 8 (over x, core), expert: 64 (over y, z).
Axes of the slice: x: 4, y: 8, z: 8, core: 2. Of those that a mesh axis runs over, the one named last changes fastest.
Arguments:
- carried: bfloat16 [8, 4096, 2048], P('section', 'expert'), may hold values from -6 to 6
- incoming: bfloat16 [1, 4096, 2048], P(None, 'expert'), may hold values from -6 to 6
- norm_gain: float32 [8, 2048], P('section'), may hold values from 0.25 to 1.75
- expert_ids: int32 [8, 2, 4096, 2], P('section', None, 'expert'), may hold values from 0 to 15, all different within a row; in each aligned block of 64 rows (0 to 63, 64 to 127, ..., all dimensions but the last counted through in order) at most 12 rows name the same one
- gate_weights: float32 [8, 2, 4096, 2], P('section', None, 'expert'), may hold values from 0.3 to 1
- w_gate: bfloat16 [8, 2048, 16384], P('section', None, 'expert'), may hold values from -0.125 to 0.125
- w_up: bfloat16 [8, 2048, 16384], P('section', None, 'expert'), may hold values from -0.125 to 0.125
- w_down: bfloat16 [8, 16384, 2048], P('section', 'expert'), may hold values from -0.1875 to 0.1875
Outputs:
- mixed: bfloat16 [8, 4096, 2048], P('section', 'expert')
Inputs may be any that keep to these rules, and one draw needn't show every extreme that they name: `expert_ids`: in each aligned block of 64 rows (the tokens of one device for one section and step) every row names 2 different experts, and no expert is named by more than 12 rows; in some block some expert is named by exactly 12 rows.
All inputs are finite; a program needn't handle non-finite values.
Results may differ from a plain program's by a relative error of at most 0.007.
Values may be sent and summed in bfloat16 or wider, within the bound.
A program may use at most 64 MiB of HBM per device.

v0:
```python
import jax
import jax.numpy as jnp
from jax import lax
from jax.sharding import PartitionSpec as P

EXPERTS = 16
TOP = 2
STEPS = 2
CAP = 12


def passed_along(shard, axis, by):
    length = lax.axis_size(axis)
    pairs = [(i, i + by) for i in range(length) if 0 <= i + by < length]
    return lax.ppermute(shard, axis, pairs)


def expert_rows(token_rows, gate_mat, up_mat, down_mat):
    gate_act = jnp.dot(token_rows, gate_mat, preferred_element_type=jnp.float32)
    up_act = jnp.dot(token_rows, up_mat, preferred_element_type=jnp.float32)
    hidden = (jax.nn.silu(gate_act) * up_act).astype(jnp.bfloat16)
    return jnp.dot(hidden, down_mat, preferred_element_type=jnp.float32).astype(jnp.bfloat16)


def moe_layer(token_block, norm_scale, route_ids, gate_vals, gate_mat, up_mat, down_mat):
    split_count = lax.axis_size("expert") // EXPERTS
    tok_count = token_block.shape[0]
    width = token_block.shape[1]
    x_float = token_block.astype(jnp.float32)
    normed = (
        x_float
        * lax.rsqrt(jnp.mean(x_float * x_float, axis=-1, keepdims=True) + 1e-06)
        * norm_scale
    ).astype(jnp.bfloat16)
    slot_ids = route_ids.reshape(-1)
    onehot = (slot_ids[:, None] == jnp.arange(EXPERTS, dtype=jnp.int32)[None, :]).astype(jnp.int32)
    before = jnp.cumsum(onehot, axis=0) - onehot
    position = jnp.sum(before * onehot, axis=1)
    target = slot_ids * CAP + position
    slot_table = target[:, None] == jnp.arange(EXPERTS * CAP, dtype=jnp.int32)[None, :]
    placement = jnp.sum(
        slot_table.astype(jnp.bfloat16).reshape(tok_count, TOP, EXPERTS * CAP), axis=1
    )
    send_rows = jnp.dot(placement.T, normed, preferred_element_type=jnp.float32).astype(
        jnp.bfloat16
    )
    outgoing = jnp.repeat(send_rows.reshape(EXPERTS, CAP, width), split_count, axis=0)
    arrived = lax.all_to_all(outgoing, "expert", split_axis=0, concat_axis=0, tiled=True)
    partials = expert_rows(arrived.reshape(-1, width), gate_mat, up_mat, down_mat).reshape(
        arrived.shape
    )
    returned = lax.all_to_all(partials, "expert", split_axis=0, concat_axis=0, tiled=True)
    expert_sum = jnp.sum(
        returned.reshape(EXPERTS, split_count, CAP, width).astype(jnp.float32), axis=1
    )
    expert_sum = expert_sum.reshape(EXPERTS * CAP, width)
    weighted = jnp.where(
        target[:, None] == jnp.arange(EXPERTS * CAP, dtype=jnp.int32)[None, :],
        gate_vals.reshape(-1)[:, None],
        0.0,
    )
    mix_table = jnp.sum(weighted.reshape(tok_count, TOP, EXPERTS * CAP), axis=1)
    branch = jnp.dot(
        mix_table, expert_sum, precision=lax.Precision.HIGHEST, preferred_element_type=jnp.float32
    )
    return (x_float + branch).astype(jnp.bfloat16)


def on_device(carried, incoming, norm_gain, expert_ids, gate_weights, w_gate, w_up, w_down):
    section_index = lax.axis_index("section")
    state = carried[0]
    layer_out = state
    for step_index in range(STEPS):
        layer_out = moe_layer(
            state,
            norm_gain[0],
            expert_ids[0, step_index],
            gate_weights[0, step_index],
            w_gate[0],
            w_up[0],
            w_down[0],
        )
        if step_index + 1 < STEPS:
            passed = passed_along(layer_out, "section", 1)
            state = jnp.where(section_index == 0, incoming[step_index], passed)
    return layer_out[None]


def solution(mesh):
    return jax.shard_map(
        on_device,
        mesh=mesh,
        in_specs=(
            P("section", "expert", None),
            P(None, "expert", None),
            P("section", None),
            P("section", None, "expert", None),
            P("section", None, "expert", None),
            P("section", None, "expert"),
            P("section", None, "expert"),
            P("section", "expert", None),
        ),
        out_specs=P("section", "expert", None),
        check_vma=False,
    )
```

profile of v0, /device:TPU:74, one launch (start us, length us, event | category | flops | bytes accessed | tf_op | source)
XLA Modules:
  0.0 618.0 jit_solution(7521472173529006720)
XLA Ops:
  0.0 0.8 fusion.48
  2.6 0.7 bitcast_add_fusion.1
  3.4 1.1 fusion.28
  4.5 1.4 convolution_convert_fusion.3
  5.9 0.2 reshape.126
  6.1 0.5 broadcast_in_dim.46
  6.6 114.7 %all_to_all.20 = bf16[64,12,2048]{2,1,0:T(8,128)(2,1)} all-to-all(bf16[64,12,2048]{2,1,0:T(8,128)(2,1)S(1)} %bitcast.61), channel_id=1, replica_groups=mesh['section'=8,'expert'=64] {'expert'}, dimensions={0} | all-to-all | bytes 6291456 | tf_op jit(solution)/shard_map/all_to_all | solution.py:48
  121.3 6.3 %reshape.128 = bf16[768,2048]{1,0:T(8,128)(2,1)} reshape(bf16[64,12,2048]{2,1,0:T(8,128)(2,1)} %all_to_all.20) | data formatting | bytes 6291456 | tf_op jit(solution)/shard_map/reshape | solution.py:49
  127.6 3.8 fusion.13
  131.4 7.1 %convolution_convert_fusion.1 = bf16[768,2048]{1,0:T(8,128)(2,1)} fusion(bf16[768,2048]{1,0:T(8,128)(2,1)} %reshape.128, bf16[1,256,2048]{2,1,0:T(8,128)(2,1)S(1)} %copy-done, bf16[1,2048,256]{2,1,0:T(8,128)(2,1)S(1)} %copy-done.6, f32[768,256]{1,0:T(8,128)} %fusion.13), kind=kOutput, calls=%fused_computation.3 | convolution fusion | flops 1613365248 | bytes 9175040 | tf_op jit(solution)/shard_map/dot_general | solution.py:22
  138.6 6.1 reshape.129
  144.7 21.6 %all-to-all-start.1 = ((bf16[64,12,2048]{2,1,0:T(8,128)(2,1)}), bf16[64,12,2048]{2,1,0:T(8,128)(2,1)}, u32[]{:S(2)}, u32[]{:S(2)}) async-start(bf16[64,12,2048]{2,1,0:T(8,128)(2,1)} %reshape.129), calls=%async_computation.1 | async-start | bytes 8388608 | tf_op jit(solution)/shard_map/all_to_all | solution.py:52
  166.4 122.4 %all-to-all-done.1 = bf16[64,12,2048]{2,1,0:T(8,128)(2,1)} async-done(((bf16[64,12,2048]{2,1,0:T(8,128)(2,1)}), bf16[64,12,2048]{2,1,0:T(8,128)(2,1)}, u32[]{:S(2)}, u32[]{:S(2)}) %all-to-all-start.1) | async-done | bytes 3145760 | tf_op jit(solution)/shard_map/all_to_all | solution.py:52
  288.8 3.2 convert_reduce_fusion.1
  292.0 1.3 reshape.130
  293.3 2.5 fusion
  295.8 1.9 collective-permute-start
  297.9 5.7 collective-permute-done
  303.5 1.1 fusion.25
  304.7 0.4 convolution_convert_fusion.2
  305.1 0.2 reshape.131
  305.3 0.5 broadcast_in_dim.49
  305.8 137.7 %all_to_all.21 = bf16[64,12,2048]{2,1,0:T(8,128)(2,1)} all-to-all(bf16[64,12,2048]{2,1,0:T(8,128)(2,1)S(1)} %bitcast.62), channel_id=1, replica_groups=mesh['section'=8,'expert'=64] {'expert'}, dimensions={0} | all-to-all | bytes 6291456 | tf_op jit(solution)/shard_map/all_to_all | solution.py:48
  443.6 6.3 %reshape.133 = bf16[768,2048]{1,0:T(8,128)(2,1)} reshape(bf16[64,12,2048]{2,1,0:T(8,128)(2,1)} %all_to_all.21) | data formatting | bytes 6291456 | tf_op jit(solution)/shard_map/reshape | solution.py:49
  449.8 3.8 fusion.11
  453.7 7.1 %convolution_convert_fusion = bf16[768,2048]{1,0:T(8,128)(2,1)} fusion(bf16[768,2048]{1,0:T(8,128)(2,1)} %reshape.133, bf16[1,256,2048]{2,1,0:T(8,128)(2,1)S(1)} %copy-done, bf16[1,2048,256]{2,1,0:T(8,128)(2,1)S(1)} %copy-done.7, f32[768,256]{1,0:T(8,128)} %fusion.11), kind=kOutput, calls=%fused_computation.2 | convolution fusion | flops 1613365248 | bytes 9175040 | tf_op jit(solution)/shard_map/dot_general | solution.py:22
  460.8 6.1 reshape.134
  466.9 12.5 %all-to-all-start.3 = ((bf16[64,12,2048]{2,1,0:T(8,128)(2,1)}), bf16[64,12,2048]{2,1,0:T(8,128)(2,1)}, u32[]{:S(2)}, u32[]{:S(2)}) async-start(bf16[64,12,2048]{2,1,0:T(8,128)(2,1)} %reshape.134), calls=%async_computation.3 | async-start | bytes 8388608 | tf_op jit(solution)/shard_map/all_to_all | solution.py:52
  479.4 130.8 %all-to-all-done.3 = bf16[64,12,2048]{2,1,0:T(8,128)(2,1)} async-done(((bf16[64,12,2048]{2,1,0:T(8,128)(2,1)}), bf16[64,12,2048]{2,1,0:T(8,128)(2,1)}, u32[]{:S(2)}, u32[]{:S(2)}) %all-to-all-start.3) | async-done | bytes 3145760 | tf_op jit(solution)/shard_map/all_to_all | solution.py:52
  610.2 3.2 convert_reduce_fusion
  613.4 1.3 reshape.135
  614.8 3.2 fusion.2
  (37 shorter events, 2.2 us)
Async XLA Ops:
  0.0 131.4 %copy-start = (bf16[1,256,2048]{2,1,0:T(8,128)(2,1)S(1)}, bf16[1,256,2048]{2,1,0:T(8,128)(2,1)}, u32[]{:S(2)}) copy-start(bf16[1,256,2048]{2,1,0:T(8,128)(2,1)} %param.15) | copy-start | bytes 3145732
  121.3 6.3 %copy-start.4 = (bf16[1,2048,256]{2,1,0:T(8,128)(2,1)S(1)}, bf16[1,2048,256]{2,1,0:T(8,128)(2,1)}, u32[]{:S(2)}) copy-start(bf16[1,2048,256]{2,1,0:T(8,128)(2,1)} %param.13) | copy-start | bytes 3145732
  127.6 3.8 copy-start.6
  144.6 21.6 %copy-start.3 = (f32[1,2,64,2]{2,3,1,0:T(2,128)S(1)}, f32[1,2,64,2]{2,3,1,0:T(2,128)}, u32[]{:S(2)}) copy-start(f32[1,2,64,2]{2,3,1,0:T(2,128)} %param.12) | copy-start | bytes 3076
  144.7 144.1 %all-to-all-start.1 = ((bf16[64,12,2048]{2,1,0:T(8,128)(2,1)}), bf16[64,12,2048]{2,1,0:T(8,128)(2,1)}, u32[]{:S(2)}, u32[]{:S(2)}) async-start(bf16[64,12,2048]{2,1,0:T(8,128)(2,1)} %reshape.129), calls=%async_computation.1 | async-start | bytes 8388608 | tf_op jit(solution)/shard_map/all_to_all | solution.py:52
  292.0 1.4 copy-start.1
  292.0 12.7 %copy-start.2 = (f32[1,2048]{1,0:T(1,128)S(1)}, f32[1,2048]{1,0:T(1,128)}, u32[]{:S(2)}) copy-start(f32[1,2048]{1,0:T(1,128)} %param.10) | copy-start | bytes 24580
  295.8 7.7 %collective-permute-start = (bf16[64,2048]{1,0:T(8,128)(2,1)S(1)}, bf16[64,2048]{1,0:T(8,128)(2,1)S(1)}, u32[]{:S(2)}, u32[]{:S(2)}) collective-permute-start(bf16[64,2048]{1,0:T(8,128)(2,1)S(1)} %fusion), channel_id=1, source_target_pairs={{0,64},{64,128},{128,192},{192,256},{256,320},{320,384},{384,448},... | collective-permute-start | bytes 786440 | tf_op jit(solution)/shard_map/ppermute | solution.py:15
  443.6 6.3 %copy-start.5 = (bf16[1,2048,256]{2,1,0:T(8,128)(2,1)S(1)}, bf16[1,2048,256]{2,1,0:T(8,128)(2,1)}, u32[]{:S(2)}) copy-start(bf16[1,2048,256]{2,1,0:T(8,128)(2,1)} %param.13) | copy-start | bytes 3145732
  449.8 3.8 copy-start.7
  466.9 143.4 %all-to-all-start.3 = ((bf16[64,12,2048]{2,1,0:T(8,128)(2,1)}), bf16[64,12,2048]{2,1,0:T(8,128)(2,1)}, u32[]{:S(2)}, u32[]{:S(2)}) async-start(bf16[64,12,2048]{2,1,0:T(8,128)(2,1)} %reshape.134), calls=%async_computation.3 | async-start | bytes 8388608 | tf_op jit(solution)/shard_map/all_to_all | solution.py:52
where the time goes:
time: 619 us; the launch traced here: 618 us
  waiting for transfers between devices  259 us (42%)
  blocking collectives  252 us (41%)
  starting transfers between devices  36 us (6%)
  local copies, waits for them, and re-layouts  30.4 us (5%)
  matrix products  29.4 us (5%)
  other arithmetic  10.6 us (2%)
    all_to_all x2, waiting for transfers between devices, moe_layer(): lax.all_to_all(partials, 'expert', split_axis=0, concat_axis=0, tiled=True)  253 us
    all_to_all x2, blocking collectives, moe_layer(): lax.all_to_all(outgoing, 'expert', split_axis=0, concat_axis=0, tiled=True)  252 us
    all_to_all x2, starting transfers between devices, moe_layer(): lax.all_to_all(partials, 'expert', split_axis=0, concat_axis=0, tiled=True)  34 us
    dot_general x2, matrix products, expert_rows(): jnp.dot(hidden, down_mat, preferred_element_type=jnp.float32)  14.3 us
    reshape x2, local copies, waits for them, and re-layouts, moe_layer(): arrived.reshape(-1, width)  12.5 us
  transfers between devices with their start and end apart: 3, of which 3 were waited for; matrix products, arithmetic and copies ran while one was open for 0% of the time, Pallas kernels for 0%

commit v1 on v0

v1 whole, which is shorter than its diff:
```python
import jax
import jax.numpy as jnp
from jax import lax
from jax.experimental import pallas as pl
from jax.experimental.pallas import tpu as pltpu
from jax.sharding import PartitionSpec as P

EXPERTS = 16
TOP = 2
STEPS = 2
CAP = 12
SPLIT = 4
RING = 8
PAIRS = RING // 2
MESH = pl.DeviceIdType.MESH


def routing(ids, gates):
    steps, tokens, _ = ids.shape
    flat = ids.reshape(steps, tokens * TOP)
    onehot = (flat[..., None] == jnp.arange(EXPERTS, dtype=jnp.int32)).astype(jnp.float32)
    below = jnp.tril(jnp.ones((tokens * TOP, tokens * TOP), jnp.float32), -1)
    before = jnp.einsum("ij,sje->sie", below, onehot, preferred_element_type=jnp.float32)
    position = jnp.sum(before * onehot, axis=-1)
    target = (flat.astype(jnp.float32) * CAP + position).reshape(steps, tokens, TOP)
    rows = jnp.concatenate([target, gates], axis=-1)
    rows = jnp.swapaxes(rows, 1, 2)
    rows = jnp.concatenate([rows, rows], axis=-1)
    return jnp.pad(rows, ((0, 0), (0, 4), (0, 0)))


def kernel(
    carried_ref, incoming_ref, gain_ref, meta_ref, wg_hbm, wu_hbm, wd_hbm,
    out_ref,
    state, tokens, meta, sent, rows, hidden, back, returned, part, parts, wg, wu, wd,
    w_sem, meta_ssem, meta_rsem, wd_ssem, wd_rsem,
    ring_ssem, ring_rsem, row_ssem, row_rsem, hid_ssem, hid_rsem,
    back_ssem, back_rsem, part_ssem, part_rsem, pass_ssem, pass_rsem,
):
    section = lax.axis_index("section")
    sections = lax.axis_size("section")
    me = lax.axis_index("expert")
    y, z = me // RING, me % RING
    half, q = z // SPLIT, z % SPLIT
    own = z // 2
    tok = carried_ref.shape[0]
    width = carried_ref.shape[1]
    slot = 2 * CAP
    cols = wd.shape[2]

    def at(yy, zz):
        return {"expert": yy * RING + zz}

    def remote(src, dst, ssem, rsem, device):
        return pltpu.make_async_remote_copy(
            src_ref=src, dst_ref=dst, send_sem=ssem, recv_sem=rsem, device_id=device, device_id_type=MESH
        )

    load_g = pltpu.make_async_copy(wg_hbm, wg, w_sem.at[0])
    load_u = pltpu.make_async_copy(wu_hbm, wu, w_sem.at[1])
    load_d = pltpu.make_async_copy(wd_hbm.at[:, pl.ds(pl.multiple_of(q * cols, cols), cols)], wd.at[q], w_sem.at[2])
    load_g.start()
    load_u.start()
    load_d.start()

    barrier = pltpu.get_barrier_semaphore()
    for d in range(1, RING):
        pl.semaphore_signal(barrier, inc=1, device_id=at(y, (z + d) % RING), device_id_type=MESH)
        pl.semaphore_signal(barrier, inc=1, device_id=at((y + d) % RING, z), device_id_type=MESH)

    @pl.when(section > 0)
    def _():
        pl.semaphore_signal(barrier, inc=1, device_id={"section": section - 1}, device_id_type=MESH)

    @pl.when(section < sections - 1)
    def _():
        pl.semaphore_signal(barrier, inc=1, device_id={"section": section + 1}, device_id_type=MESH)

    state[0] = carried_ref[...]
    linked = (section > 0).astype(jnp.int32) + (section < sections - 1).astype(jnp.int32)
    pl.semaphore_wait(barrier, 2 * (RING - 1) + linked)

    def meta_copy(d):
        return remote(meta_ref, meta.at[z], meta_ssem.at[d], meta_rsem.at[d], at(y, (z + d) % RING))

    meta_local = pltpu.make_async_copy(meta_ref, meta.at[z], meta_rsem.at[0])
    meta_local.start()
    for d in (1, 7, 2, 6, 3, 5, 4):
        meta_copy(d).start()

    def down_copy(d):
        other = (q + d) % SPLIT
        return remote(
            wd_hbm.at[:, pl.ds(pl.multiple_of(other * cols, cols), cols)], wd.at[q],
            wd_ssem.at[d], wd_rsem.at[d], at(y, half * SPLIT + other),
        )

    row_id = lax.broadcasted_iota(jnp.int32, (RING, slot, 2 * tok), 1)
    dest_id = lax.broadcasted_iota(jnp.int32, (RING, slot, 2 * tok), 0)
    lane_id = lax.broadcasted_iota(jnp.int32, (RING, slot, 2 * tok), 2)
    row_odd = (row_id >= CAP).astype(jnp.int32)
    lane_odd = (lane_id >= tok).astype(jnp.int32)
    key = dest_id * slot + half * CAP + row_id - CAP * row_odd
    key = jnp.where(row_odd == lane_odd, key, -1).astype(jnp.float32).reshape(RING * slot, 2 * tok)
    low_lane = lax.broadcasted_iota(jnp.int32, (1, 2 * tok), 1) < tok

    def step(st, carry):
        @pl.when(st == 1)
        def _():
            @pl.when(section == 0)
            def _():
                state[1] = incoming_ref[...]

            @pl.when(section > 0)
            def _():
                remote(out_ref, state.at[1], pass_ssem, pass_rsem, {"section": section}).wait_recv()

        x = state[st].astype(jnp.float32)
        scale = lax.rsqrt(jnp.mean(x * x, axis=-1, keepdims=True) + 1e-06)
        tokens[st, z] = (x * scale * gain_ref[...]).astype(jnp.bfloat16)

        def ring_copy(way, hop):
            sign = 1 - 2 * way
            origin = (z - sign * (hop - 1) + RING) % RING
            block = tokens.at[st, origin]
            if hop == RING // 2:
                block = block.at[pl.ds(way * (tok // 2), tok // 2)]
            return remote(
                block, block, ring_ssem.at[way, hop - 1], ring_rsem.at[st, way, hop - 1], at(y, (z + sign + RING) % RING)
            )

        def hop(n):
            for way in range(2):
                ring_copy(way, n).wait_recv()
                if n < RING // 2:
                    ring_copy(way, n + 1).start()

        def lanes(pair, row):
            return jnp.where(low_lane, meta[2 * pair, st, row : row + 1, :], meta[2 * pair + 1, st, row : row + 1, :])

        def row_copy(pair, d):
            dest = (y + d) % RING
            return remote(
                sent.at[pair, dest], rows.at[st, pair, y], row_ssem.at[pair, d], row_rsem.at[st, pair, d], at(dest, z)
            )

        def row_local(pair):
            return pltpu.make_async_copy(sent.at[pair, y], rows.at[st, pair, y], row_rsem.at[st, pair, 0])

        def select(pair):
            pick = ((key == lanes(pair, 0)) | (key == lanes(pair, 1))).astype(jnp.bfloat16)
            block = tokens[st, pl.ds(2 * pair, 2)].reshape(2 * tok, width)
            for c in range(0, width, 512):
                got = jnp.dot(pick, block[:, c : c + 512], preferred_element_type=jnp.float32)
                sent[pair, :, :, c : c + 512] = got.astype(jnp.bfloat16).reshape(RING, slot, 512)
            for d in (4, 3, 5, 2, 6, 1, 7):
                row_copy(pair, d).start()
            row_local(pair).start()

        def hidden_copy(pair, d):
            return remote(
                hidden.at[st, pair, q], hidden.at[st, pair, q], hid_ssem.at[pair, d], hid_rsem.at[st, pair, d],
                at(y, half * SPLIT + (q + d) % SPLIT),
            )

        def forward(pair):
            row_local(pair).wait()
            for d in range(1, RING):
                row_copy(pair, d).wait_recv()
            arrived = rows[st, pair].reshape(RING * slot, width)
            gate = jnp.dot(arrived, wg[...], preferred_element_type=jnp.float32)
            up = jnp.dot(arrived, wu[...], preferred_element_type=jnp.float32)
            act = gate / (1.0 + jnp.exp(-gate)) * up
            hidden[st, pair, q] = act.astype(jnp.bfloat16)
            for d in (1, 3, 2):
                hidden_copy(pair, d).start()

        def back_copy(pair, d):
            dest = (y + d) % RING
            return remote(
                back.at[pair, dest], returned.at[st, pair, y], back_ssem.at[pair, d], back_rsem.at[st, pair, d], at(dest, z)
            )

        def back_local(pair):
            return pltpu.make_async_copy(back.at[pair, y], returned.at[st, pair, y], back_rsem.at[st, pair, 0])

        def down(pair):
            for d in range(1, SPLIT):
                hidden_copy(pair, d).wait_recv()
            total = jnp.dot(hidden[st, pair, 0], wd[0], preferred_element_type=jnp.float32)
            for k in range(1, SPLIT):
                total += jnp.dot(hidden[st, pair, k], wd[k], preferred_element_type=jnp.float32)
            back[pair] = total.astype(jnp.bfloat16).reshape(RING, slot, cols)
            for d in (4, 3, 5, 2, 6, 1, 7):
                back_copy(pair, d).start()
            back_local(pair).start()

        def part_copy(pair, b):
            dest = 2 * pair + b
            return remote(
                part.at[pair, b], parts.at[st, z], part_ssem.at[pair, b], part_rsem.at[st, (dest - z + RING) % RING], at(y, dest)
            )

        def part_local(pair, b):
            return pltpu.make_async_copy(part.at[pair, b], parts.at[st, z], part_rsem.at[st, 0])

        def combine(pair):
            back_local(pair).wait()
            for d in range(1, RING):
                back_copy(pair, d).wait_recv()
            mix = jnp.where(key == lanes(pair, 0), lanes(pair, 2), 0.0) + jnp.where(key == lanes(pair, 1), lanes(pair, 3), 0.0)
            high = mix.astype(jnp.bfloat16)
            low = (mix - high.astype(jnp.float32)).astype(jnp.bfloat16)
            values = returned[st, pair].reshape(RING * slot, cols)
            dims = (((0,), (0,)), ((), ()))
            total = lax.dot_general(high, values, dims, preferred_element_type=jnp.float32)
            total += lax.dot_general(low, values, dims, preferred_element_type=jnp.float32)
            part[pair] = total.astype(jnp.bfloat16).reshape(2, tok, cols)
            for b in range(2):
                @pl.when(2 * pair + b == z)
                def _():
                    part_local(pair, b).start()

                @pl.when(2 * pair + b != z)
                def _():
                    part_copy(pair, b).start()

        mine, sibling = own, half * 2 + (1 - own % 2)
        first, second = half * 2, half * 2 + 1
        third, fourth = (half * 2 + 2) % PAIRS, (half * 2 + 3) % PAIRS

        for way in range(2):
            ring_copy(way, 1).start()

        @pl.when(st == 0)
        def _():
            for d in range(1, SPLIT):
                down_copy(d).start()
            meta_local.wait()
            for d in range(1, RING):
                meta_copy(d).wait_recv()

        hop(1)
        select(mine)
        hop(2)
        hop(3)
        select(sibling)
        hop(4)
        select(third)
        select(fourth)

        @pl.when(st == 0)
        def _():
            load_g.wait()
            load_u.wait()

        forward(mine)
        forward(sibling)

        @pl.when(st == 0)
        def _():
            load_d.wait()
            for d in range(1, SPLIT):
                down_copy(d).wait_recv()

        down(first)
        down(second)
        combine(first)
        combine(second)
        forward(third)
        down(third)
        combine(third)
        forward(fourth)
        down(fourth)
        combine(fourth)

        part_own = pltpu.make_async_copy(part.at[0, 0], parts.at[st, z], part_rsem.at[st, 0])
        part_own.wait()
        for d in range(1, RING):
            remote(part.at[0, 0], parts.at[st, z], part_ssem.at[0, 0], part_rsem.at[st, d], at(y, z)).wait_recv()
        for k in range(SPLIT):
            span = slice(k * cols, (k + 1) * cols)
            total = parts[st, k].astype(jnp.float32) + parts[st, SPLIT + k].astype(jnp.float32)
            out_ref[:, span] = (state[st, :, span].astype(jnp.float32) + total).astype(jnp.bfloat16)

        pass_on = remote(out_ref, state.at[1], pass_ssem, pass_rsem, {"section": section + 1})

        @pl.when((st == 0) & (section < sections - 1))
        def _():
            pass_on.start()

        for way in range(2):
            for n in range(1, RING // 2 + 1):
                ring_copy(way, n).wait_send()
        for pair in range(PAIRS):
            for d in range(1, RING):
                row_copy(pair, d).wait_send()
                back_copy(pair, d).wait_send()
            for d in range(1, SPLIT):
                hidden_copy(pair, d).wait_send()
            for b in range(2):
                @pl.when(2 * pair + b != z)
                def _():
                    part_copy(pair, b).wait_send()

        @pl.when((st == 0) & (section < sections - 1))
        def _():
            pass_on.wait_send()

        return carry

    lax.fori_loop(0, STEPS, step, 0)
    for d in range(1, RING):
        meta_copy(d).wait_send()
    for d in range(1, SPLIT):
        down_copy(d).wait_send()


def on_device(carried, incoming, norm_gain, expert_ids, gate_weights, w_gate, w_up, w_down):
    meta = routing(expert_ids[0], gate_weights[0])
    tok, width = carried.shape[1:]
    units = w_gate.shape[2]
    cols = width // SPLIT
    slot = 2 * CAP
    lanes = meta.shape[-1]
    bf16 = jnp.bfloat16
    dma = pltpu.SemaphoreType.DMA
    vmem = pl.BlockSpec(memory_space=pltpu.VMEM)
    hbm = pl.BlockSpec(memory_space=pl.ANY)
    out = pl.pallas_call(
        kernel,
        out_shape=jax.ShapeDtypeStruct((tok, width), bf16),
        in_specs=[vmem] * 4 + [hbm] * 3,
        out_specs=vmem,
        scratch_shapes=[
            pltpu.VMEM((STEPS, tok, width), bf16),
            pltpu.VMEM((STEPS, RING, tok, width), bf16),
            pltpu.VMEM((RING, STEPS, 8, lanes), jnp.float32),
            pltpu.VMEM((PAIRS, RING, slot, width), bf16),
            pltpu.VMEM((STEPS, PAIRS, RING, slot, width), bf16),
            pltpu.VMEM((STEPS, PAIRS, SPLIT, RING * slot, units), bf16),
            pltpu.VMEM((PAIRS, RING, slot, cols), bf16),
            pltpu.VMEM((STEPS, PAIRS, RING, slot, cols), bf16),
            pltpu.VMEM((PAIRS, 2, tok, cols), bf16),
            pltpu.VMEM((STEPS, RING, tok, cols), bf16),
            pltpu.VMEM((width, units), bf16),
            pltpu.VMEM((width, units), bf16),
            pltpu.VMEM((SPLIT, units, cols), bf16),
            dma((3,)), dma((RING,)), dma((RING,)), dma((SPLIT,)), dma((SPLIT,)),
            dma((2, 4)), dma((STEPS, 2, 4)),
            dma((PAIRS, RING)), dma((STEPS, PAIRS, RING)),
            dma((PAIRS, SPLIT)), dma((STEPS, PAIRS, SPLIT)),
            dma((PAIRS, RING)), dma((STEPS, PAIRS, RING)),
            dma((PAIRS, 2)), dma((STEPS, RING)),
            dma, dma,
        ],
        compiler_params=pltpu.CompilerParams(
            collective_id=0, has_side_effects=True, vmem_limit_bytes=48 * 1024 * 1024
        ),
    )(carried[0], incoming[0], norm_gain, meta, w_gate[0], w_up[0], w_down[0])
    return out[None]


def solution(mesh):
    return jax.shard_map(
        on_device,
        mesh=mesh,
        in_specs=(
            P("section", "expert", None),
            P(None, "expert", None),
            P("section", None),
            P("section", None, "expert", None),
            P("section", None, "expert", None),
            P("section", None, "expert"),
            P("section", None, "expert"),
            P("section", "expert", None),
        ),
        out_specs=P("section", "expert", None),
        check_vma=False,
    )
```

time: 619 us -> 306 us (0.49)
  the two profiles are of different devices: /device:TPU:74 before, /device:TPU:6 now
where the time goes in v1:
time: 306 us; the launch traced here: 304 us
  Pallas kernels  295 us (96%)
  local copies, waits for them, and re-layouts  8.42 us (3%)
    pallas_call x1, Pallas kernels, on_device(): pl.pallas_call(kernel, out_shape=jax.ShapeDtypeStruct((tok, width), bf16)...  295 us
    unnamed x18, local copies, waits for them, and re-layouts  8.03 us

profile of v1, /device:TPU:6, one launch (start us, length us, event | category | flops | bytes accessed | tf_op | source)
XLA Modules:
  0.0 303.8 jit_solution(16427817876292722508)
XLA Ops:
  0.0 0.0 copy-start.3
  0.0 0.8 copy.9
  0.8 0.1 eq.15
  1.0 0.2 fusion.1
  1.2 0.2 reduce_sum.12
  1.4 0.0 copy-start.6
  1.4 0.1 copy.10
  1.5 0.6 copy-done.6
  2.0 0.0 copy-start.7
  2.1 0.7 copy-done.7
  2.7 0.0 copy-start.5
  2.7 0.1 select_maximum_fusion.meta_ref
  2.8 0.0 copy-done.3
  2.8 0.6 copy-done.5
  3.4 0.0 copy-start
  3.4 1.2 copy-done
  4.7 0.0 copy-start.1
  4.7 1.2 copy-done.1
  5.9 0.0 copy-start.2
  5.9 1.2 copy-done.2
  7.1 0.0 copy-start.4
  7.1 0.9 copy-done.4
  8.1 295.0 %shard_map.82 = bf16[64,2048]{1,0:T(8,128)(2,1)S(1)} custom-call(bf16[64,2048]{1,0:T(8,128)(2,1)S(1)} %bitcast.26, bf16[64,2048]{1,0:T(8,128)(2,1)S(1)} %bitcast.27, f32[1,2048]{1,0:T(1,128)S(1)} %copy-done.5, f32[2,8,128]{2,1,0:T(8,128)S(1)} %select_maximum_fusion.meta_ref, bf16[2048,256]{1,0:T(8,128)(2,1)S(1)} %bitcast.22, bf16[2048,256]{1,0:T(8,128)(2,1)S(1)} %bitcast.23, ...), custom_call_target="tpu_custom_call" | custom-call | tf_op jit(solution)/shard_map/pallas_call | solution.py:330
  303.1 0.7 copy.12
  (3 shorter events, 0.0 us)
Async XLA Ops:
  0.0 2.8 copy-start.3
  1.4 0.7 copy-start.6
  2.0 0.7 copy-start.7
  2.7 0.7 copy-start.5
  3.4 1.2 copy-start
  4.7 1.2 copy-start.1
  5.9 1.2 copy-start.2
  7.1 0.9 copy-start.4

commit v2 on v1

--- a/solution.py
+++ b/solution.py
@@ -13,28 +13,37 @@
 RING = 8
 PAIRS = RING // 2
 MESH = pl.DeviceIdType.MESH
-
-
-def routing(ids, gates):
-    steps, tokens, _ = ids.shape
-    flat = ids.reshape(steps, tokens * TOP)
-    onehot = (flat[..., None] == jnp.arange(EXPERTS, dtype=jnp.int32)).astype(jnp.float32)
-    below = jnp.tril(jnp.ones((tokens * TOP, tokens * TOP), jnp.float32), -1)
-    before = jnp.einsum("ij,sje->sie", below, onehot, preferred_element_type=jnp.float32)
-    position = jnp.sum(before * onehot, axis=-1)
-    target = (flat.astype(jnp.float32) * CAP + position).reshape(steps, tokens, TOP)
-    rows = jnp.concatenate([target, gates], axis=-1)
-    rows = jnp.swapaxes(rows, 1, 2)
-    rows = jnp.concatenate([rows, rows], axis=-1)
-    return jnp.pad(rows, ((0, 0), (0, 4), (0, 0)))
+NEAR_ONE = True
+FAR_FIRST = (4, 3, 5, 2, 6, 1, 7)
+
+
+def routing(st, ids_ref, gates_ref, meta_ref):
+    twice = lambda row: jnp.concatenate([row, row], axis=1)
+    tok = ids_ref.shape[2]
+    first, second = twice(ids_ref[st, 0:1, :]), twice(ids_ref[st, 1:2, :])
+    expert = lax.broadcasted_iota(jnp.int32, (EXPERTS, 2 * tok), 0)
+    lane = lax.broadcasted_iota(jnp.int32, (2 * tok, 2 * tok), 1)
+    ahead = lax.broadcasted_iota(jnp.int32, (2 * tok, 2 * tok), 0) < lane - jnp.where(lane >= tok, tok, 0)
+    ahead = ahead.astype(jnp.bfloat16)
+    in_first = (expert == first).astype(jnp.float32)
+    in_second = (expert == second).astype(jnp.float32)
+    count = lambda hot: jnp.dot(hot.astype(jnp.bfloat16), ahead, preferred_element_type=jnp.float32)
+    total = 0.5 * jnp.sum(in_first, axis=1, keepdims=True)
+    place_first = jnp.sum(in_first * count(in_first), axis=0, keepdims=True)
+    place_second = jnp.sum(in_second * (count(in_second) + total), axis=0, keepdims=True)
+    meta_ref[st, 0:1, :] = first.astype(jnp.float32) * CAP + place_first
+    meta_ref[st, 1:2, :] = second.astype(jnp.float32) * CAP + place_second
+    meta_ref[st, 2:3, :] = twice(gates_ref[st, 0:1, :])
+    meta_ref[st, 3:4, :] = twice(gates_ref[st, 1:2, :])
+    meta_ref[st, 4:8, :] = jnp.zeros((4, 2 * tok), jnp.float32)
 
 
 def kernel(
-    carried_ref, incoming_ref, gain_ref, meta_ref, wg_hbm, wu_hbm, wd_hbm,
+    carried_ref, incoming_ref, gain_ref, ids_ref, gates_ref, wg_hbm, wu_hbm, wd_hbm,
     out_ref,
-    state, tokens, meta, sent, rows, hidden, back, returned, part, parts, wg, wu, wd,
+    state, tokens, meta_ref, meta, sent, rows, sent_one, rows_one, hidden, back, returned, part, parts, wg, wu, wd,
     w_sem, meta_ssem, meta_rsem, wd_ssem, wd_rsem,
-    ring_ssem, ring_rsem, row_ssem, row_rsem, hid_ssem, hid_rsem,
+    ring_ssem, ring_rsem, row_ssem, row_rsem, one_ssem, one_rsem, relay_ssem, relay_rsem, hid_ssem, hid_rsem,
     back_ssem, back_rsem, part_ssem, part_rsem, pass_ssem, pass_rsem,
 ):
     section = lax.axis_index("section")
@@ -43,10 +52,17 @@
     y, z = me // RING, me % RING
     half, q = z // SPLIT, z % SPLIT
     own = z // 2
+    par = z % 2
+    mate = z + 1 - 2 * par
+    peer = q + 1 - 2 * par
+    inner = 1 + q // 2
+    other = 2 - q // 2
+    other_outer = 3 - 3 * (q // 2)
     tok = carried_ref.shape[0]
     width = carried_ref.shape[1]
     slot = 2 * CAP
     cols = wd.shape[2]
+    span = width // 2
 
     def at(yy, zz):
         return {"expert": yy * RING + zz}
@@ -77,6 +93,8 @@
         pl.semaphore_signal(barrier, inc=1, device_id={"section": section + 1}, device_id_type=MESH)
 
     state[0] = carried_ref[...]
+    for st in range(STEPS):
+        routing(st, ids_ref, gates_ref, meta_ref)
     linked = (section > 0).astype(jnp.int32) + (section < sections - 1).astype(jnp.int32)
     pl.semaphore_wait(barrier, 2 * (RING - 1) + linked)
 
@@ -102,6 +120,7 @@
     lane_odd = (lane_id >= tok).astype(jnp.int32)
     key = dest_id * slot + half * CAP + row_id - CAP * row_odd
     key = jnp.where(row_odd == lane_odd, key, -1).astype(jnp.float32).reshape(RING * slot, 2 * tok)
+    odd_row = lax.broadcasted_iota(jnp.int32, (RING, slot, wg.shape[1]), 1).reshape(RING * slot, wg.shape[1]) >= CAP
     low_lane = lax.broadcasted_iota(jnp.int32, (1, 2 * tok), 1) < tok
 
     def step(st, carry):
@@ -138,42 +157,104 @@
         def lanes(pair, row):
             return jnp.where(low_lane, meta[2 * pair, st, row : row + 1, :], meta[2 * pair + 1, st, row : row + 1, :])
 
-        def row_copy(pair, d):
+        def row_copy(n, d):
             dest = (y + d) % RING
-            return remote(
-                sent.at[pair, dest], rows.at[st, pair, y], row_ssem.at[pair, d], row_rsem.at[st, pair, d], at(dest, z)
-            )
-
-        def row_local(pair):
-            return pltpu.make_async_copy(sent.at[pair, y], rows.at[st, pair, y], row_rsem.at[st, pair, 0])
-
-        def select(pair):
+            return remote(sent.at[n, dest], rows.at[st, n, y], row_ssem.at[n, d], row_rsem.at[st, n, d], at(dest, z))
+
+        def row_local(n):
+            return pltpu.make_async_copy(sent.at[n, y], rows.at[st, n, y], row_rsem.at[st, n, 0])
+
+        def select(n, pair):
             pick = ((key == lanes(pair, 0)) | (key == lanes(pair, 1))).astype(jnp.bfloat16)
             block = tokens[st, pl.ds(2 * pair, 2)].reshape(2 * tok, width)
             for c in range(0, width, 512):
                 got = jnp.dot(pick, block[:, c : c + 512], preferred_element_type=jnp.float32)
-                sent[pair, :, :, c : c + 512] = got.astype(jnp.bfloat16).reshape(RING, slot, 512)
-            for d in (4, 3, 5, 2, 6, 1, 7):
-                row_copy(pair, d).start()
-            row_local(pair).start()
-
-        def hidden_copy(pair, d):
+                sent[n, :, :, c : c + 512] = got.astype(jnp.bfloat16).reshape(RING, slot, 512)
+            for d in FAR_FIRST:
+                row_copy(n, d).start()
+            row_local(n).start()
+
+        def one_place(i):
+            return rows_one.at[st, (0, 0, 1, 2)[i], 1 - par if i == 1 else par]
+
+        def one_copy(i, d):
+            dest = (y + d) % RING
             return remote(
-                hidden.at[st, pair, q], hidden.at[st, pair, q], hid_ssem.at[pair, d], hid_rsem.at[st, pair, d],
-                at(y, half * SPLIT + (q + d) % SPLIT),
+                sent_one.at[i, dest], one_place(i).at[y], one_ssem.at[i, d], one_rsem.at[st, i, d], at(dest, z)
             )
 
-        def forward(pair):
-            row_local(pair).wait()
+        def one_local(i):
+            return pltpu.make_async_copy(sent_one.at[i, y], one_place(i).at[y], one_rsem.at[st, i, 0])
+
+        def select_one(i, column):
+            pick = (key == meta[column, st, 0:1, :]) | (key == meta[column, st, 1:2, :])
+            block = jnp.concatenate([tokens[st, column, :, :span], tokens[st, column, :, span:]], axis=0)
+            for c in range(0, span, 512):
+                got = jnp.dot(pick.astype(jnp.bfloat16), block[:, c : c + 512], preferred_element_type=jnp.float32)
+                sent_one[i, :, :, c : c + 512] = got.astype(jnp.bfloat16).reshape(RING, slot, 512)
+            for d in FAR_FIRST:
+                one_copy(i, d).start()
+            one_local(i).start()
+
+        def one_wait(i, d):
+            if d == 0:
+                one_local(i).wait()
+            else:
+                one_copy(i, d).wait_recv()
+
+        def relay_copy(c, d, mine):
+            place = rows_one.at[st, c, par if mine else 1 - par, (y - d + RING) % RING]
+            return remote(place, place, relay_ssem.at[c - 1, d], relay_rsem.at[st, c - 1, d], at(y, mate))
+
+        def relay(c):
+            for d in (0, 1, 7, 2, 6, 3, 5, 4):
+                one_wait(c + 1, d)
+                relay_copy(c, d, True).start()
+
+        def hidden_copy(pair, source, k, device):
+            block = hidden.at[st, pair, source]
+            return remote(block, block, hid_ssem.at[pair, k], hid_rsem.at[st, pair, source], at(y, half * SPLIT + device))
+
+        def hidden_pass(pair):
+            @pl.when(inner == q)
+            def _():
+                for k, source in enumerate((other, other_outer)):
+                    hidden_copy(pair, source, 2 + k, q).wait_recv()
+                    hidden_copy(pair, source, 2 + k, peer).start()
+
+        def share(pair, gate, up):
+            act = gate / (1.0 + jnp.exp(-gate)) * up
+            hidden[st, pair, q] = act.astype(jnp.bfloat16)
+            hidden_copy(pair, q, 0, other).start()
+            hidden_copy(pair, q, 1, peer).start()
+
+        def forward(n, pair):
+            row_local(n).wait()
             for d in range(1, RING):
-                row_copy(pair, d).wait_recv()
-            arrived = rows[st, pair].reshape(RING * slot, width)
+                row_copy(n, d).wait_recv()
+            arrived = rows[st, n].reshape(RING * slot, width)
             gate = jnp.dot(arrived, wg[...], preferred_element_type=jnp.float32)
             up = jnp.dot(arrived, wu[...], preferred_element_type=jnp.float32)
-            act = gate / (1.0 + jnp.exp(-gate)) * up
-            hidden[st, pair, q] = act.astype(jnp.bfloat16)
-            for d in (1, 3, 2):
-                hidden_copy(pair, d).start()
+            share(pair, gate, up)
+
+        def forward_one(c, pair):
+            for d in range(RING):
+                if c == 0:
+                    one_wait(0, d)
+                    one_wait(1, d)
+                else:
+                    relay_copy(c, d, False).wait_recv()
+            even = rows_one[st, c, 0].reshape(RING * slot, span)
+            odd = rows_one[st, c, 1].reshape(RING * slot, span)
+
+            def project(w):
+                top, bottom = w[:span], w[span:]
+                dot = lambda a, b: jnp.dot(a, b, preferred_element_type=jnp.float32)
+                from_even = dot(even, top) + pltpu.roll(dot(even, bottom), RING * slot - CAP, 0)
+                from_odd = pltpu.roll(dot(odd, top), CAP, 0) + dot(odd, bottom)
+                return jnp.where(odd_row, from_odd, from_even)
+
+            share(pair, project(wg), project(wu))
 
         def back_copy(pair, d):
             dest = (y + d) % RING
@@ -185,8 +266,13 @@
             return pltpu.make_async_copy(back.at[pair, y], returned.at[st, pair, y], back_rsem.at[st, pair, 0])
 
         def down(pair):
-            for d in range(1, SPLIT):
-                hidden_copy(pair, d).wait_recv()
+            hidden_copy(pair, peer, 0, q).wait_recv()
+
+            @pl.when(inner != q)
+            def _():
+                for source in (other, other_outer):
+                    hidden_copy(pair, source, 0, q).wait_recv()
+
             total = jnp.dot(hidden[st, pair, 0], wd[0], preferred_element_type=jnp.float32)
             for k in range(1, SPLIT):
                 total += jnp.dot(hidden[st, pair, k], wd[k], preferred_element_type=jnp.float32)
@@ -225,7 +311,7 @@
                 def _():
                     part_copy(pair, b).start()
 
-        mine, sibling = own, half * 2 + (1 - own % 2)
+        sibling, near, far = own + 1 - 2 * (own % 2), PAIRS - 1 - own, (own + 2) % PAIRS
         first, second = half * 2, half * 2 + 1
         third, fourth = (half * 2 + 2) % PAIRS, (half * 2 + 3) % PAIRS
 
@@ -234,28 +320,56 @@
 
         @pl.when(st == 0)
         def _():
+            meta_local.wait()
+
+        select_one(0, z)
+
+        @pl.when(st == 0)
+        def _():
+            for d in (1, 7):
+                meta_copy(d).wait_recv()
+
+        hop(1)
+        select_one(1, mate)
+
+        @pl.when(st == 0)
+        def _():
+            for d in range(2, 7):
+                meta_copy(d).wait_recv()
+
+        hop(2)
+        select_one(2, 2 * sibling + par)
+        if NEAR_ONE:
+            select_one(3, 2 * near + par)
+
+        @pl.when(st == 0)
+        def _():
+            load_g.wait()
+            load_u.wait()
+
+        forward_one(0, own)
+        hop(3)
+
+        @pl.when(st == 0)
+        def _():
             for d in range(1, SPLIT):
                 down_copy(d).start()
-            meta_local.wait()
-            for d in range(1, RING):
-                meta_copy(d).wait_recv()
-
-        hop(1)
-        select(mine)
-        hop(2)
-        hop(3)
-        select(sibling)
+
+        if not NEAR_ONE:
+            select(0, near)
+        relay(1)
         hop(4)
-        select(third)
-        select(fourth)
-
-        @pl.when(st == 0)
-        def _():
-            load_g.wait()
-            load_u.wait()
-
-        forward(mine)
-        forward(sibling)
+        select(1, far)
+
+        if NEAR_ONE:
+            relay(2)
+        forward_one(1, sibling)
+        hidden_pass(first)
+        hidden_pass(second)
+        if NEAR_ONE:
+            forward_one(2, near)
+        else:
+            forward(0, near)
 
         @pl.when(st == 0)
         def _():
@@ -265,13 +379,14 @@
 
         down(first)
         down(second)
+        forward(1, far)
         combine(first)
         combine(second)
-        forward(third)
+        hidden_pass(third)
+        hidden_pass(fourth)
         down(third)
+        down(fourth)
         combine(third)
-        forward(fourth)
-        down(fourth)
         combine(fourth)
 
         part_own = pltpu.make_async_copy(part.at[0, 0], parts.at[st, z], part_rsem.at[st, 0])
@@ -279,9 +394,9 @@
         for d in range(1, RING):
             remote(part.at[0, 0], parts.at[st, z], part_ssem.at[0, 0], part_rsem.at[st, d], at(y, z)).wait_recv()
         for k in range(SPLIT):
-            span = slice(k * cols, (k + 1) * cols)
+            block = slice(k * cols, (k + 1) * cols)
             total = parts[st, k].astype(jnp.float32) + parts[st, SPLIT + k].astype(jnp.float32)
-            out_ref[:, span] = (state[st, :, span].astype(jnp.float32) + total).astype(jnp.bfloat16)
+            out_ref[:, block] = (state[st, :, block].astype(jnp.float32) + total).astype(jnp.bfloat16)
 
         pass_on = remote(out_ref, state.at[1], pass_ssem, pass_rsem, {"section": section + 1})
 
@@ -292,12 +407,25 @@
         for way in range(2):
             for n in range(1, RING // 2 + 1):
                 ring_copy(way, n).wait_send()
+        for d in range(1, RING):
+            for n in range(1 if NEAR_ONE else 0, 2):
+                row_copy(n, d).wait_send()
+            for i in range(4 if NEAR_ONE else 3):
+                one_copy(i, d).wait_send()
+        for c in range(1, 3 if NEAR_ONE else 2):
+            for d in range(RING):
+                relay_copy(c, d, True).wait_send()
         for pair in range(PAIRS):
             for d in range(1, RING):
-                row_copy(pair, d).wait_send()
                 back_copy(pair, d).wait_send()
-            for d in range(1, SPLIT):
-                hidden_copy(pair, d).wait_send()
+            hidden_copy(pair, q, 0, other).wait_send()
+            hidden_copy(pair, q, 1, peer).wait_send()
+
+            @pl.when(inner == q)
+            def _():
+                for k, source in enumerate((other, other_outer)):
+                    hidden_copy(pair, source, 2 + k, peer).wait_send()
+
             for b in range(2):
                 @pl.when(2 * pair + b != z)
                 def _():
@@ -317,12 +445,12 @@
 
 
 def on_device(carried, incoming, norm_gain, expert_ids, gate_weights, w_gate, w_up, w_down):
-    meta = routing(expert_ids[0], gate_weights[0])
+    ids, gates = jnp.swapaxes(expert_ids[0], 1, 2), jnp.swapaxes(gate_weights[0], 1, 2)
     tok, width = carried.shape[1:]
     units = w_gate.shape[2]
     cols = width // SPLIT
     slot = 2 * CAP
-    lanes = meta.shape[-1]
+    lanes = 2 * tok
     bf16 = jnp.bfloat16
     dma = pltpu.SemaphoreType.DMA
     vmem = pl.BlockSpec(memory_space=pltpu.VMEM)
@@ -330,14 +458,17 @@
     out = pl.pallas_call(
         kernel,
         out_shape=jax.ShapeDtypeStruct((tok, width), bf16),
-        in_specs=[vmem] * 4 + [hbm] * 3,
+        in_specs=[vmem] * 5 + [hbm] * 3,
         out_specs=vmem,
         scratch_shapes=[
             pltpu.VMEM((STEPS, tok, width), bf16),
             pltpu.VMEM((STEPS, RING, tok, width), bf16),
+            pltpu.VMEM((STEPS, 8, lanes), jnp.float32),
             pltpu.VMEM((RING, STEPS, 8, lanes), jnp.float32),
-            pltpu.VMEM((PAIRS, RING, slot, width), bf16),
-            pltpu.VMEM((STEPS, PAIRS, RING, slot, width), bf16),
+            pltpu.VMEM((2, RING, slot, width), bf16),
+            pltpu.VMEM((STEPS, 2, RING, slot, width), bf16),
+            pltpu.VMEM((4, RING, slot, width // 2), bf16),
+            pltpu.VMEM((STEPS, 3, 2, RING, slot, width // 2), bf16),
             pltpu.VMEM((STEPS, PAIRS, SPLIT, RING * slot, units), bf16),
             pltpu.VMEM((PAIRS, RING, slot, cols), bf16),
             pltpu.VMEM((STEPS, PAIRS, RING, slot, cols), bf16),
@@ -348,16 +479,18 @@
             pltpu.VMEM((SPLIT, units, cols), bf16),
             dma((3,)), dma((RING,)), dma((RING,)), dma((SPLIT,)), dma((SPLIT,)),
             dma((2, 4)), dma((STEPS, 2, 4)),
-            dma((PAIRS, RING)), dma((STEPS, PAIRS, RING)),
+            dma((2, RING)), dma((STEPS, 2, RING)),
+            dma((4, RING)), dma((STEPS, 4, RING)),
+            dma((2, RING)), dma((STEPS, 2, RING)),
             dma((PAIRS, SPLIT)), dma((STEPS, PAIRS, SPLIT)),
             dma((PAIRS, RING)), dma((STEPS, PAIRS, RING)),
             dma((PAIRS, 2)), dma((STEPS, RING)),
             dma, dma,
         ],
         compiler_params=pltpu.CompilerParams(
-            collective_id=0, has_side_effects=True, vmem_limit_bytes=48 * 1024 * 1024
+            collective_id=0, has_side_effects=True, vmem_limit_bytes=62 * 1024 * 1024
         ),
-    )(carried[0], incoming[0], norm_gain, meta, w_gate[0], w_up[0], w_down[0])
+    )(carried[0], incoming[0], norm_gain, ids, gates, w_gate[0], w_up[0], w_down[0])
     return out[None]
 
 

time: 306 us -> 217 us (0.71)
  Pallas kernels: 295 us -> 213 us
  local copies, waits for them, and re-layouts: 8.42 us -> 1.67 us
    pallas_call x1, Pallas kernels: 295 us -> 213 us  [on_device(): pl.pallas_call(kernel, out_shape=jax.ShapeDtypeStruct((tok, width), bf16)...]
    unnamed x18 -> x1, local copies, waits for them, and re-layouts: 8.03 us -> 1.67 us
where the time goes in v2:
time: 217 us; the launch traced here: 214 us
  Pallas kernels  213 us (98%)
    pallas_call x1, Pallas kernels, on_device(): pl.pallas_call(kernel, out_shape=jax.ShapeDtypeStruct((tok, width), bf16)...  213 us

profile of v2, /device:TPU:6, one launch (start us, length us, event | category | flops | bytes accessed | tf_op | source)
XLA Modules:
  0.0 214.3 jit_solution(5372629014181744615)
XLA Ops:
  0.0 212.6 %shard_map.82 = bf16[64,2048]{1,0:T(8,128)(2,1)} custom-call(bf16[64,2048]{1,0:T(8,128)(2,1)} %bitcast.16, bf16[64,2048]{1,0:T(8,128)(2,1)} %bitcast.17, f32[1,2048]{1,0:T(1,128)} %gain_ref.1, s32[2,2,64]{2,1,0:T(2,128)} %bitcast.18, f32[2,2,64]{2,1,0:T(2,128)} %bitcast.19, bf16[2048,256]{1,0:T(8,128)(2,1)} %bitcast.12, bf16[2048,256]{1,0:T(8,128)(2,1)} %bitcast.13, ...), custom_call_target="tpu_custom_call" | custom-call | tf_op jit(solution)/shard_map/pallas_call | solution.py:458
  212.6 1.7 copy.10

commit v3 on v2

--- a/solution.py
+++ b/solution.py
@@ -55,7 +55,6 @@
     par = z % 2
     mate = z + 1 - 2 * par
     peer = q + 1 - 2 * par
-    inner = 1 + q // 2
     other = 2 - q // 2
     other_outer = 3 - 3 * (q // 2)
     tok = carried_ref.shape[0]
@@ -140,19 +139,26 @@
 
         def ring_copy(way, hop):
             sign = 1 - 2 * way
-            origin = (z - sign * (hop - 1) + RING) % RING
-            block = tokens.at[st, origin]
-            if hop == RING // 2:
-                block = block.at[pl.ds(way * (tok // 2), tok // 2)]
+            block = tokens.at[st, (z - sign * (hop - 1) + RING) % RING]
             return remote(
                 block, block, ring_ssem.at[way, hop - 1], ring_rsem.at[st, way, hop - 1], at(y, (z + sign + RING) % RING)
             )
 
         def hop(n):
             for way in range(2):
-                ring_copy(way, n).wait_recv()
-                if n < RING // 2:
+                if n < RING // 2 - 1:
+                    ring_copy(way, n).wait_recv()
                     ring_copy(way, n + 1).start()
+                elif n < RING // 2:
+                    ring_copy(way, n).wait_recv()
+
+                    @pl.when(par == 1 - way)
+                    def _():
+                        ring_copy(way, n + 1).start()
+                else:
+                    @pl.when(par == way)
+                    def _():
+                        ring_copy(way, n).wait_recv()
 
         def lanes(pair, row):
             return jnp.where(low_lane, meta[2 * pair, st, row : row + 1, :], meta[2 * pair + 1, st, row : row + 1, :])
@@ -207,26 +213,20 @@
             return remote(place, place, relay_ssem.at[c - 1, d], relay_rsem.at[st, c - 1, d], at(y, mate))
 
         def relay(c):
-            for d in (0, 1, 7, 2, 6, 3, 5, 4):
+            for d in (0,) + FAR_FIRST:
                 one_wait(c + 1, d)
                 relay_copy(c, d, True).start()
 
         def hidden_copy(pair, source, k, device):
             block = hidden.at[st, pair, source]
             return remote(block, block, hid_ssem.at[pair, k], hid_rsem.at[st, pair, source], at(y, half * SPLIT + device))
-
-        def hidden_pass(pair):
-            @pl.when(inner == q)
-            def _():
-                for k, source in enumerate((other, other_outer)):
-                    hidden_copy(pair, source, 2 + k, q).wait_recv()
-                    hidden_copy(pair, source, 2 + k, peer).start()
 
         def share(pair, gate, up):
             act = gate / (1.0 + jnp.exp(-gate)) * up
             hidden[st, pair, q] = act.astype(jnp.bfloat16)
             hidden_copy(pair, q, 0, other).start()
             hidden_copy(pair, q, 1, peer).start()
+            hidden_copy(pair, q, 2, other_outer).start()
 
         def forward(n, pair):
             row_local(n).wait()
@@ -267,12 +267,8 @@
 
         def down(pair):
             hidden_copy(pair, peer, 0, q).wait_recv()
-
-            @pl.when(inner != q)
-            def _():
-                for source in (other, other_outer):
-                    hidden_copy(pair, source, 0, q).wait_recv()
-
+            for source in (other, other_outer):
+                hidden_copy(pair, source, 0, q).wait_recv()
             total = jnp.dot(hidden[st, pair, 0], wd[0], preferred_element_type=jnp.float32)
             for k in range(1, SPLIT):
                 total += jnp.dot(hidden[st, pair, k], wd[k], preferred_element_type=jnp.float32)
@@ -364,8 +360,6 @@
         if NEAR_ONE:
             relay(2)
         forward_one(1, sibling)
-        hidden_pass(first)
-        hidden_pass(second)
         if NEAR_ONE:
             forward_one(2, near)
         else:
@@ -382,8 +376,6 @@
         forward(1, far)
         combine(first)
         combine(second)
-        hidden_pass(third)
-        hidden_pass(fourth)
         down(third)
         down(fourth)
         combine(third)
@@ -405,8 +397,13 @@
             pass_on.start()
 
         for way in range(2):
-            for n in range(1, RING // 2 + 1):
+            for n in range(1, RING // 2):
                 ring_copy(way, n).wait_send()
+
+            @pl.when(par == 1 - way)
+            def _():
+                ring_copy(way, RING // 2).wait_send()
+
         for d in range(1, RING):
             for n in range(1 if NEAR_ONE else 0, 2):
                 row_copy(n, d).wait_send()
@@ -416,16 +413,12 @@
             for d in range(RING):
                 relay_copy(c, d, True).wait_send()
         for pair in range(PAIRS):
+            hidden_copy(pair, q, 0, other).wait_send()
+            hidden_copy(pair, q, 1, peer).wait_send()
+            hidden_copy(pair, q, 2, other_outer).wait_send()
+        for pair in range(PAIRS):
             for d in range(1, RING):
                 back_copy(pair, d).wait_send()
-            hidden_copy(pair, q, 0, other).wait_send()
-            hidden_copy(pair, q, 1, peer).wait_send()
-
-            @pl.when(inner == q)
-            def _():
-                for k, source in enumerate((other, other_outer)):
-                    hidden_copy(pair, source, 2 + k, peer).wait_send()
-
             for b in range(2):
                 @pl.when(2 * pair + b != z)
                 def _():

time: 217 us -> 209 us (0.963)
  Pallas kernels: 213 us -> 206 us
    pallas_call x1, Pallas kernels: 213 us -> 206 us  [on_device(): pl.pallas_call(kernel, out_shape=jax.ShapeDtypeStruct((tok, width), bf16)...]
where the time goes in v3:
time: 209 us; the launch traced here: 208 us
  Pallas kernels  206 us (99%)
    pallas_call x1, Pallas kernels, on_device(): pl.pallas_call(kernel, out_shape=jax.ShapeDtypeStruct((tok, width), bf16)...  206 us

profile of v3, /device:TPU:6, one launch (start us, length us, event | category | flops | bytes accessed | tf_op | source)
XLA Modules:
  0.0 207.9 jit_solution(8234139617029542415)
XLA Ops:
  0.0 206.2 %shard_map.82 = bf16[64,2048]{1,0:T(8,128)(2,1)} custom-call(bf16[64,2048]{1,0:T(8,128)(2,1)} %bitcast.16, bf16[64,2048]{1,0:T(8,128)(2,1)} %bitcast.17, f32[1,2048]{1,0:T(1,128)} %gain_ref.1, s32[2,2,64]{2,1,0:T(2,128)} %bitcast.18, f32[2,2,64]{2,1,0:T(2,128)} %bitcast.19, bf16[2048,256]{1,0:T(8,128)(2,1)} %bitcast.12, bf16[2048,256]{1,0:T(8,128)(2,1)} %bitcast.13, ...), custom_call_target="tpu_custom_call" | custom-call | tf_op jit(solution)/shard_map/pallas_call | solution.py:451
  206.2 1.7 copy.10

commit v4 on v3

--- a/solution.py
+++ b/solution.py
@@ -14,7 +14,7 @@
 PAIRS = RING // 2
 MESH = pl.DeviceIdType.MESH
 NEAR_ONE = True
-FAR_FIRST = (4, 3, 5, 2, 6, 1, 7)
+NEAR_FIRST = (1, 7, 2, 6, 3, 5, 4)
 
 
 def routing(st, ids_ref, gates_ref, meta_ref):
@@ -176,7 +176,7 @@
             for c in range(0, width, 512):
                 got = jnp.dot(pick, block[:, c : c + 512], preferred_element_type=jnp.float32)
                 sent[n, :, :, c : c + 512] = got.astype(jnp.bfloat16).reshape(RING, slot, 512)
-            for d in FAR_FIRST:
+            for d in NEAR_FIRST:
                 row_copy(n, d).start()
             row_local(n).start()
 
@@ -198,7 +198,7 @@
             for c in range(0, span, 512):
                 got = jnp.dot(pick.astype(jnp.bfloat16), block[:, c : c + 512], preferred_element_type=jnp.float32)
                 sent_one[i, :, :, c : c + 512] = got.astype(jnp.bfloat16).reshape(RING, slot, 512)
-            for d in FAR_FIRST:
+            for d in NEAR_FIRST:
                 one_copy(i, d).start()
             one_local(i).start()
 
@@ -213,7 +213,7 @@
             return remote(place, place, relay_ssem.at[c - 1, d], relay_rsem.at[st, c - 1, d], at(y, mate))
 
         def relay(c):
-            for d in (0,) + FAR_FIRST:
+            for d in (0,) + NEAR_FIRST:
                 one_wait(c + 1, d)
                 relay_copy(c, d, True).start()
 

time: 209 us -> 210 us (level)
  no operation moved by 1% of the time
where the time goes in v4:
time: 210 us
  Pallas kernels  208 us (99%)
    pallas_call x1, Pallas kernels, on_device(): pl.pallas_call(kernel, out_shape=jax.ShapeDtypeStruct((tok, width), bf16)...  208 us

profile of v4, /device:TPU:6, one launch (start us, length us, event | category | flops | bytes accessed | tf_op | source)
XLA Modules:
  0.0 209.6 jit_solution(8128677359610253013)
XLA Ops:
  0.0 207.9 %shard_map.82 = bf16[64,2048]{1,0:T(8,128)(2,1)} custom-call(bf16[64,2048]{1,0:T(8,128)(2,1)} %bitcast.16, bf16[64,2048]{1,0:T(8,128)(2,1)} %bitcast.17, f32[1,2048]{1,0:T(1,128)} %gain_ref.1, s32[2,2,64]{2,1,0:T(2,128)} %bitcast.18, f32[2,2,64]{2,1,0:T(2,128)} %bitcast.19, bf16[2048,256]{1,0:T(8,128)(2,1)} %bitcast.12, bf16[2048,256]{1,0:T(8,128)(2,1)} %bitcast.13, ...), custom_call_target="tpu_custom_call" | custom-call | tf_op jit(solution)/shard_map/pallas_call | solution.py:451
  207.9 1.7 copy.10
